TPU v7x, 256 devices: a whole 4x4x8 slice. The times are simulated.
256 devices in a mesh: samp: 16 (over z, core), feat: 16 (over x, y).
Axes of the slice: x: 4, y: 4, z: 8, core: 2. Of those that a mesh axis runs over, the one named last changes fastest.
Arguments:
- differences: bfloat16 [9216, 131072], P('samp', 'feat'), may hold values from -600 to 600
- start_block: bfloat16 [64, 131072], P(None, 'feat'), may hold values from -6 to 6
Outputs:
- directions: float32 [64, 131072], P(None, 'feat')
- layer_scores: float32 [16, 64], P('feat')
All inputs are finite; a program needn't handle non-finite values.
Results may differ from a plain program's by a relative error of at most 0.0043.
Values may be sent and summed in bfloat16 or wider, within the bound.
A program may use at most 64 MiB of HBM per device.

v0:
```python
import math
import jax
import jax.numpy as jnp
from jax import lax
from jax.sharding import PartitionSpec as P

WIDTH = 8192
ITERS = 2
FEATURES = 131072


def orthonormal(pulled, gram):
    lower = jnp.linalg.cholesky(gram)
    return lax.linalg.triangular_solve(lower, pulled, left_side=True, lower=True)


def on_device(differences, start_block):
    block = start_block
    basis = None
    for step in range(ITERS):
        partial_rows = lax.dot_general(
            block, differences, (((1,), (1,)), ((), ())), preferred_element_type=jnp.float32
        )
        projected = lax.psum(partial_rows, "feat").astype(jnp.bfloat16)
        partial_cols = jnp.dot(projected, differences, preferred_element_type=jnp.float32)
        pulled = lax.psum(partial_cols, "samp")
        local_gram = jnp.dot(pulled, pulled.T, precision=lax.Precision.HIGHEST)
        gram = lax.psum(local_gram, "feat")
        basis = orthonormal(pulled, gram)
        block = basis.astype(jnp.bfloat16)
    directions = basis * math.sqrt(FEATURES)
    samples = differences.shape[0]
    layers_here = differences.shape[1] // WIDTH
    stacked = differences.reshape(samples, layers_here, WIDTH)
    block_layers = block.reshape(block.shape[0], layers_here, WIDTH)
    along = jnp.einsum("kjw,sjw->jks", block_layers, stacked, preferred_element_type=jnp.float32)
    captured = jnp.sum(along * along, axis=2)
    energy = jnp.einsum("sjw,sjw->j", stacked, stacked, preferred_element_type=jnp.float32)
    captured, energy = lax.psum((captured, energy), "samp")
    layer_scores = FEATURES * captured / (energy[:, None] + 1e-06)
    return (directions, layer_scores)


def solution(mesh):
    in_specs = (P("samp", "feat"), P(None, "feat"))
    out_specs = (P(None, "feat"), P("feat", None))
    return jax.shard_map(
        on_device, mesh=mesh, in_specs=in_specs, out_specs=out_specs, check_vma=False
    )
```

profile of v0, /device:TPU:1, one launch (start us, length us, event | category | flops | bytes accessed | tf_op | source)
XLA Modules:
  0.0 635.0 jit_solution(9600654586622632830)
XLA Ops:
  7.2 0.0 copy-start
  7.2 0.0 all-reduce.6.cloned.1.call-start
  7.2 1.2 copy-done
  8.4 6.6 %fusion.16 = f32[64,576]{1,0:T(8,128)S(1)} fusion(bf16[64,8192]{1,0:T(8,128)(2,1)S(1)} %copy-done, bf16[576,8192]{1,0:T(8,128)(2,1)} %param.5), kind=kOutput, calls=%fused_computation.30 | convolution fusion | flops 603979776 | bytes 10633216 | tf_op jit(solution)/shard_map/dot_general | solution.py:21
  15.0 63.0 %all-reduce.9 = bf16[64,576]{1,0:T(8,128)(2,1)S(1)} all-reduce(f32[64,576]{1,0:T(8,128)S(1)} %fusion.16), channel_id=1, replica_groups=mesh['samp'=16,'feat'=16] {'feat'}, use_global_device_ids=true, to_apply=%region_0.0 | all-reduce | flops 36864 | bytes 221184 | tf_op jit(solution)/shard_map/psum | solution.py:24
  77.9 6.9 %fusion.21 = f32[64,8192]{1,0:T(8,128)} fusion(bf16[64,576]{1,0:T(8,128)(2,1)S(1)} %all-reduce.9, bf16[576,8192]{1,0:T(8,128)(2,1)} %param.5), kind=kOutput, calls=%fused_computation.35 | convolution fusion | flops 603979776 | bytes 11608064 | tf_op jit(solution)/shard_map/dot_general | solution.py:25
  84.9 0.0 all-reduce.6.cloned.1.call-update
  84.9 0.0 all-reduce.8.cloned.1.call-start
  84.9 127.8 %all-reduce.6.cloned.1.call-done = f32[64,8192]{1,0:T(8,128)} async-done(((f32[64,8192]{1,0:T(8,128)}), f32[64,8192]{1,0:T(8,128)}) %all-reduce.6.cloned.1.call-update) | async-done | bytes 2097168 | tf_op jit(solution)/shard_map/psum | solution.py:26
  212.7 0.0 copy-start.2
  212.7 4.2 fusion.17
  216.9 60.3 %psum.58 = f32[64,64]{0,1:T(8,128)S(1)} all-reduce(f32[64,64]{0,1:T(8,128)S(1)} %fusion.17), channel_id=1, replica_groups=mesh['samp'=16,'feat'=16] {'feat'}, use_global_device_ids=true, to_apply=%region_2.0 | all-reduce | flops 4096 | bytes 32768 | tf_op jit(solution)/shard_map/psum | solution.py:28
  277.1 0.1 copy.5
  277.2 5.8 cholesky.44
  283.1 0.6 compare_reduce_fusion.1
  283.8 0.7 fusion.7
  284.4 4.9 custom-call.6
  289.3 0.0 copy-done.2
  289.3 1.9 convolution_convert_fusion
  291.2 6.6 %fusion.18 = f32[64,576]{1,0:T(8,128)S(1)} fusion(bf16[64,8192]{1,0:T(8,128)(2,1)S(1)} %convolution_convert_fusion, bf16[576,8192]{1,0:T(8,128)(2,1)} %param.5), kind=kOutput, calls=%fused_computation.32 | convolution fusion | flops 603979776 | bytes 10633216 | tf_op jit(solution)/shard_map/dot_general | solution.py:21
  297.8 57.4 %all-reduce.10 = bf16[64,576]{1,0:T(8,128)(2,1)S(1)} all-reduce(f32[64,576]{1,0:T(8,128)S(1)} %fusion.18), channel_id=1, replica_groups=mesh['samp'=16,'feat'=16] {'feat'}, use_global_device_ids=true, to_apply=%region_5.8 | all-reduce | flops 36864 | bytes 221184 | tf_op jit(solution)/shard_map/psum | solution.py:24
  355.3 6.9 %fusion.20 = f32[64,8192]{1,0:T(8,128)} fusion(bf16[64,576]{1,0:T(8,128)(2,1)S(1)} %all-reduce.10, bf16[576,8192]{1,0:T(8,128)(2,1)} %param.5), kind=kOutput, calls=%fused_computation.34 | convolution fusion | flops 603979776 | bytes 11608064 | tf_op jit(solution)/shard_map/dot_general | solution.py:25
  362.2 0.0 all-reduce.8.cloned.1.call-update
  362.2 9.1 %fusion = f32[]{:T(128)} fusion(bf16[576,8192]{1,0:T(8,128)(2,1)} %param.5), kind=kLoop, calls=%fused_computation.1 | loop fusion | flops 14155775 | bytes 9437188 | tf_op jit(solution)/shard_map/sjw,sjw->j/dot_general | solution.py:38
  371.4 130.6 %all-reduce.8.cloned.1.call-done = f32[64,8192]{1,0:T(8,128)} async-done(((f32[64,8192]{1,0:T(8,128)}), f32[64,8192]{1,0:T(8,128)}) %all-reduce.8.cloned.1.call-update) | async-done | bytes 2097168 | tf_op jit(solution)/shard_map/psum | solution.py:26
  502.0 0.0 copy-start.1
  502.0 4.2 fusion.19
  506.1 60.3 %psum.61 = f32[64,64]{0,1:T(8,128)S(1)} all-reduce(f32[64,64]{0,1:T(8,128)S(1)} %fusion.19), channel_id=1, replica_groups=mesh['samp'=16,'feat'=16] {'feat'}, use_global_device_ids=true, to_apply=%region_7.10 | all-reduce | flops 4096 | bytes 32768 | tf_op jit(solution)/shard_map/psum | solution.py:28
  566.4 0.1 copy.7
  566.5 5.8 cholesky.55
  572.4 0.6 compare_reduce_fusion
  573.0 0.7 fusion.8
  573.7 4.9 custom-call.7
  578.6 0.0 copy-done.1
  578.6 3.3 broadcast_multiply_fusion
  581.9 6.7 %fusion.1 = f32[64]{0:T(128)S(1)} fusion(bf16[576,8192]{1,0:T(8,128)(2,1)} %param.5, bf16[64,8192]{1,0:T(8,128)(2,1)S(1)} %get-tuple-element.7), kind=kOutput, calls=%fused_computation.4 | convolution fusion | flops 604053440 | bytes 10486016 | tf_op jit(solution)/shard_map/kjw,sjw->jks/dot_general | solution.py:36
  588.6 38.4 %all-reduce = (f32[1,64]{1,0:T(1,128)S(1)}, f32[1]{0:T(128)}) all-reduce(f32[1,64]{1,0:T(1,128)S(1)} %bitcast.39, f32[1]{0:T(128)} %bitcast.7), channel_id=1, replica_groups=mesh['samp'=16,'feat'=16] {'samp'}, use_global_device_ids=true, to_apply=%region_9.12 | all-reduce | flops 65 | bytes 520 | tf_op jit(solution)/shard_map/psum | solution.py:39
  627.6 0.5 multiply_divide_fusion
  (4 shorter events, 0.1 us)
Async XLA Ops:
  7.2 1.2 copy-start
  7.2 205.5 %all-reduce.6.cloned.1.call-start = ((), (), s32[]{:S(2)}) async-start(), calls=%async_computation | async-start | bytes 4194304 | tf_op jit(solution)/shard_map/psum | solution.py:26
  84.9 417.1 %all-reduce.8.cloned.1.call-start = ((), (), s32[]{:S(2)}) async-start(), calls=%async_computation.1 | async-start | bytes 4194304 | tf_op jit(solution)/shard_map/psum | solution.py:26
  212.7 76.6 %copy-start.2 = (f32[64,8192]{1,0:T(8,128)S(1)}, f32[64,8192]{1,0:T(8,128)}, u32[]{:S(2)}) copy-start(f32[64,8192]{1,0:T(8,128)} %all-reduce.6.cloned.1.call-done) | copy-start | bytes 6291460
  502.0 76.6 %copy-start.1 = (f32[64,8192]{1,0:T(8,128)S(1)}, f32[64,8192]{1,0:T(8,128)}, u32[]{:S(2)}) copy-start(f32[64,8192]{1,0:T(8,128)} %all-reduce.8.cloned.1.call-done) | copy-start | bytes 6291460
Sparse Core Ops, SparseCore 0:
  85.0 127.6 all-reduce.5
  362.3 139.5 all-reduce.7
where the time goes:
time: 635 us
  blocking collectives  279 us (44%)
  waiting for transfers between devices  258 us (41%)
  matrix products  47.2 us (7%)
  other arithmetic  33.8 us (5%)
  between operations  14.8 us (2%)
    psum x2, waiting for transfers between devices, on_device(): pulled = lax.psum(partial_cols, 'samp')  258 us
    psum x2, blocking collectives, on_device(): gram = lax.psum(local_gram, 'feat')  121 us
    psum x2, blocking collectives, on_device(): projected = lax.psum(partial_rows, 'feat').astype(jnp.bfloat16)  120 us
    psum x1, blocking collectives, on_device(): captured, energy = lax.psum((captured, energy), 'samp')  38.4 us
    dot_general x2, matrix products, on_device(): jnp.dot(projected, differences, preferred_element_type=jnp.float32)  13.8 us
    dot_general x2, matrix products, on_device(): lax.dot_general(block, differences, (((1,), (1,)), ((), ())), preferred_e...  13.2 us
    another operation x6, other arithmetic, orthonormal(): lower = jnp.linalg.cholesky(gram)  13 us
  transfers between devices with their start and end apart: 2, of which 2 were waited for; matrix products, arithmetic and copies ran while one was open for 1% of the time, Pallas kernels for 0%

commit v1 on v0

--- a/solution.py
+++ b/solution.py
@@ -23,7 +23,9 @@
         )
         projected = lax.psum(partial_rows, "feat").astype(jnp.bfloat16)
         partial_cols = jnp.dot(projected, differences, preferred_element_type=jnp.float32)
-        pulled = lax.psum(partial_cols, "samp")
+        pulled = partial_cols
+        for hop in (1, 2, 4, 8):
+            pulled = pulled + lax.ppermute(pulled, "samp", [(dev, dev ^ hop) for dev in range(16)])
         local_gram = jnp.dot(pulled, pulled.T, precision=lax.Precision.HIGHEST)
         gram = lax.psum(local_gram, "feat")
         basis = orthonormal(pulled, gram)

time: 635 us -> 867 us (1.37)
  waiting for transfers between devices: 258 us -> 459 us
  starting transfers between devices: 0.08 us -> 61.6 us
  between operations: 14.8 us -> 1.49 us
    ppermute x0 -> x8, waiting for transfers between devices: none -> 459 us  [on_device(): lax.ppermute(pulled, 'samp', [(dev, dev ^ hop) for dev in range(16)])]
    psum x2 -> x0, waiting for transfers between devices: 258 us -> none  [on_device(): pulled = lax.psum(partial_cols, 'samp')]
    ppermute x0 -> x8, starting transfers between devices: none -> 61.6 us  [on_device(): lax.ppermute(pulled, 'samp', [(dev, dev ^ hop) for dev in range(16)])]
  transfers between devices with their start and end apart: 2 -> 8, of which waited for: 2 -> 8; matrix products, arithmetic and copies ran while one was open for 1% -> 1% of each run, Pallas kernels for 0% -> 0%
where the time goes in v1:
time: 867 us
  waiting for transfers between devices  459 us (53%)
  blocking collectives  272 us (31%)
  starting transfers between devices  61.6 us (7%)
  matrix products  39.9 us (5%)
  other arithmetic  31.9 us (4%)
    ppermute x8, waiting for transfers between devices, on_device(): lax.ppermute(pulled, 'samp', [(dev, dev ^ hop) for dev in range(16)])  459 us
    psum x2, blocking collectives, on_device(): projected = lax.psum(partial_rows, 'feat').astype(jnp.bfloat16)  120 us
    psum x2, blocking collectives, on_device(): gram = lax.psum(local_gram, 'feat')  113 us
    ppermute x8, starting transfers between devices, on_device(): lax.ppermute(pulled, 'samp', [(dev, dev ^ hop) for dev in range(16)])  61.6 us
    psum x1, blocking collectives, on_device(): captured, energy = lax.psum((captured, energy), 'samp')  38.3 us
  transfers between devices with their start and end apart: 8, of which 8 were waited for; matrix products, arithmetic and copies ran while one was open for 1% of the time, Pallas kernels for 0%

profile of v1, /device:TPU:1, one launch (start us, length us, event | category | flops | bytes accessed | tf_op | source)
XLA Modules:
  0.0 866.5 jit_solution(13082511426058333922)
XLA Ops:
  0.6 1.2 copy-done
  1.9 6.6 fusion.16
  8.4 63.0 %all-reduce.3 = bf16[64,576]{1,0:T(8,128)(2,1)S(1)} all-reduce(f32[64,576]{1,0:T(8,128)S(1)} %fusion.16), channel_id=1, replica_groups=mesh['samp'=16,'feat'=16] {'feat'}, use_global_device_ids=true, to_apply=%region_0.0 | all-reduce | flops 36864 | bytes 221184 | tf_op jit(solution)/shard_map/psum | solution.py:24
  71.4 5.6 fusion.21
  77.0 15.0 %collective-permute-start = (f32[64,8192]{1,0:T(8,128)S(1)}, f32[64,8192]{1,0:T(8,128)S(1)}, u32[]{:S(2)}, u32[]{:S(2)}) collective-permute-start(f32[64,8192]{1,0:T(8,128)S(1)} %fusion.21), channel_id=1, source_target_pairs={{0,16},{16,0},{32,48},{48,32},{64,80},{80,64},{96,112},{112,96},{1... | collective-permute-start | bytes 6291464 | tf_op jit(solution)/shard_map/ppermute | solution.py:28
  92.0 3.8 collective-permute-done
  95.8 0.2 add.48
  96.0 1.8 collective-permute-start.1
  97.7 45.6 %collective-permute-done.1 = f32[64,8192]{1,0:T(8,128)S(1)} collective-permute-done((f32[64,8192]{1,0:T(8,128)S(1)}, f32[64,8192]{1,0:T(8,128)S(1)}, u32[]{:S(2)}, u32[]{:S(2)}) %collective-permute-start.1) | collective-permute-done | bytes 2097184 | tf_op jit(solution)/shard_map/ppermute | solution.py:28
  143.3 0.2 add.49
  143.6 3.1 collective-permute-start.2
  146.6 90.0 %collective-permute-done.2 = f32[64,8192]{1,0:T(8,128)S(1)} collective-permute-done((f32[64,8192]{1,0:T(8,128)S(1)}, f32[64,8192]{1,0:T(8,128)S(1)}, u32[]{:S(2)}, u32[]{:S(2)}) %collective-permute-start.2) | collective-permute-done | bytes 2097184 | tf_op jit(solution)/shard_map/ppermute | solution.py:28
  236.6 0.2 add.50
  236.8 6.5 collective-permute-start.3
  243.3 90.5 %collective-permute-done.3 = f32[64,8192]{1,0:T(8,128)S(1)} collective-permute-done((f32[64,8192]{1,0:T(8,128)S(1)}, f32[64,8192]{1,0:T(8,128)S(1)}, u32[]{:S(2)}, u32[]{:S(2)}) %collective-permute-start.3) | collective-permute-done | bytes 2097184 | tf_op jit(solution)/shard_map/ppermute | solution.py:28
  333.8 0.2 add.51
  334.0 1.8 fusion.17
  335.8 55.8 %psum.43 = f32[64,64]{0,1:T(8,128)S(1)} all-reduce(f32[64,64]{0,1:T(8,128)S(1)} %fusion.17), channel_id=1, replica_groups=mesh['samp'=16,'feat'=16] {'feat'}, use_global_device_ids=true, to_apply=%region_1.0 | all-reduce | flops 4096 | bytes 32768 | tf_op jit(solution)/shard_map/psum | solution.py:30
  391.7 5.8 cholesky.44
  397.6 0.6 compare_reduce_fusion.1
  398.2 0.7 fusion.7
  398.9 4.9 custom-call.6
  403.8 1.9 convolution_convert_fusion
  405.7 6.6 fusion.18
  412.3 57.2 %all-reduce.4 = bf16[64,576]{1,0:T(8,128)(2,1)S(1)} all-reduce(f32[64,576]{1,0:T(8,128)S(1)} %fusion.18), channel_id=1, replica_groups=mesh['samp'=16,'feat'=16] {'feat'}, use_global_device_ids=true, to_apply=%region_4.7 | all-reduce | flops 36864 | bytes 221184 | tf_op jit(solution)/shard_map/psum | solution.py:24
  469.5 5.7 fusion.20
  475.3 29.6 %collective-permute-start.4 = (f32[64,8192]{1,0:T(8,128)S(1)}, f32[64,8192]{1,0:T(8,128)S(1)}, u32[]{:S(2)}, u32[]{:S(2)}) collective-permute-start(f32[64,8192]{1,0:T(8,128)S(1)} %fusion.20), channel_id=1, source_target_pairs={{0,16},{16,0},{32,48},{48,32},{64,80},{80,64},{96,112},{112,96},{1... | collective-permute-start | bytes 6291464 | tf_op jit(solution)/shard_map/ppermute | solution.py:28
  504.9 3.8 collective-permute-done.4
  508.6 0.2 add.52
  509.0 46.8 %collective-permute-done.5 = f32[64,8192]{1,0:T(8,128)S(1)} collective-permute-done((f32[64,8192]{1,0:T(8,128)S(1)}, f32[64,8192]{1,0:T(8,128)S(1)}, u32[]{:S(2)}, u32[]{:S(2)}) %collective-permute-start.5) | collective-permute-done | bytes 2097184 | tf_op jit(solution)/shard_map/ppermute | solution.py:28
  555.8 0.2 add.53
  556.0 2.0 collective-permute-start.6
  558.0 91.0 %collective-permute-done.6 = f32[64,8192]{1,0:T(8,128)S(1)} collective-permute-done((f32[64,8192]{1,0:T(8,128)S(1)}, f32[64,8192]{1,0:T(8,128)S(1)}, u32[]{:S(2)}, u32[]{:S(2)}) %collective-permute-start.6) | collective-permute-done | bytes 2097184 | tf_op jit(solution)/shard_map/ppermute | solution.py:28
  649.0 0.2 add.54
  649.2 3.7 collective-permute-start.7
  652.9 5.5 fusion
  658.4 87.2 %collective-permute-done.7 = f32[64,8192]{1,0:T(8,128)S(1)} collective-permute-done((f32[64,8192]{1,0:T(8,128)S(1)}, f32[64,8192]{1,0:T(8,128)S(1)}, u32[]{:S(2)}, u32[]{:S(2)}) %collective-permute-start.7) | collective-permute-done | bytes 2097184 | tf_op jit(solution)/shard_map/ppermute | solution.py:28
  745.6 0.2 add.55
  745.8 1.8 fusion.19
  747.6 57.3 %psum.45 = f32[64,64]{0,1:T(8,128)S(1)} all-reduce(f32[64,64]{0,1:T(8,128)S(1)} %fusion.19), channel_id=1, replica_groups=mesh['samp'=16,'feat'=16] {'feat'}, use_global_device_ids=true, to_apply=%region_5.8 | all-reduce | flops 4096 | bytes 32768 | tf_op jit(solution)/shard_map/psum | solution.py:30
  805.0 5.8 cholesky.55
  810.9 0.6 compare_reduce_fusion
  811.5 0.7 fusion.8
  812.2 4.9 custom-call.7
  817.1 3.3 broadcast_multiply_fusion
  820.3 6.7 fusion.1
  827.0 38.3 %all-reduce = (f32[1,64]{1,0:T(1,128)S(1)}, f32[1]{0:T(128)}) all-reduce(f32[1,64]{1,0:T(1,128)S(1)} %bitcast.41, f32[1]{0:T(128)} %bitcast.7), channel_id=1, replica_groups=mesh['samp'=16,'feat'=16] {'samp'}, use_global_device_ids=true, to_apply=%region_7.10 | all-reduce | flops 65 | bytes 520 | tf_op jit(solution)/shard_map/psum | solution.py:41
  866.0 0.5 multiply_divide_fusion
  (15 shorter events, 0.3 us)
Async XLA Ops:
  0.6 1.2 copy-start
  77.0 18.7 %collective-permute-start = (f32[64,8192]{1,0:T(8,128)S(1)}, f32[64,8192]{1,0:T(8,128)S(1)}, u32[]{:S(2)}, u32[]{:S(2)}) collective-permute-start(f32[64,8192]{1,0:T(8,128)S(1)} %fusion.21), channel_id=1, source_target_pairs={{0,16},{16,0},{32,48},{48,32},{64,80},{80,64},{96,112},{112,96},{1... | collective-permute-start | bytes 6291464 | tf_op jit(solution)/shard_map/ppermute | solution.py:28
  96.0 47.4 %collective-permute-start.1 = (f32[64,8192]{1,0:T(8,128)S(1)}, f32[64,8192]{1,0:T(8,128)S(1)}, u32[]{:S(2)}, u32[]{:S(2)}) collective-permute-start(f32[64,8192]{1,0:T(8,128)S(1)} %add.48), channel_id=1, source_target_pairs={{0,32},{16,48},{32,0},{48,16},{64,96},{80,112},{96,64},{112,80},{1... | collective-permute-start | bytes 6291464 | tf_op jit(solution)/shard_map/ppermute | solution.py:28
  143.6 93.1 %collective-permute-start.2 = (f32[64,8192]{1,0:T(8,128)S(1)}, f32[64,8192]{1,0:T(8,128)S(1)}, u32[]{:S(2)}, u32[]{:S(2)}) collective-permute-start(f32[64,8192]{1,0:T(8,128)S(1)} %add.49), channel_id=1, source_target_pairs={{0,64},{16,80},{32,96},{48,112},{64,0},{80,16},{96,32},{112,48},{1... | collective-permute-start | bytes 6291464 | tf_op jit(solution)/shard_map/ppermute | solution.py:28
  236.8 96.9 %collective-permute-start.3 = (f32[64,8192]{1,0:T(8,128)S(1)}, f32[64,8192]{1,0:T(8,128)S(1)}, u32[]{:S(2)}, u32[]{:S(2)}) collective-permute-start(f32[64,8192]{1,0:T(8,128)S(1)} %add.50), channel_id=1, source_target_pairs={{0,128},{16,144},{32,160},{48,176},{64,192},{80,208},{96,224},{112... | collective-permute-start | bytes 6291464 | tf_op jit(solution)/shard_map/ppermute | solution.py:28
  469.5 183.4 %slice-start = ((s8[9437184]{0:T(1024)(128)(4,1)}), s8[4194304]{0:T(1024)(128)(4,1)S(1)}, s32[]{:S(2)}) async-start(s8[9437184]{0:T(1024)(128)(4,1)} %bitcast.39), calls=%async_computation | async-start | bytes 8388608
  469.5 183.4 %slice-start.1 = ((s8[9437184]{0:T(1024)(128)(4,1)}), s8[4194304]{0:T(1024)(128)(4,1)S(1)}, s32[]{:S(2)}) async-start(s8[9437184]{0:T(1024)(128)(4,1)} %bitcast.39), calls=%async_computation.1 | async-start | bytes 8388608
  475.3 33.4 %collective-permute-start.4 = (f32[64,8192]{1,0:T(8,128)S(1)}, f32[64,8192]{1,0:T(8,128)S(1)}, u32[]{:S(2)}, u32[]{:S(2)}) collective-permute-start(f32[64,8192]{1,0:T(8,128)S(1)} %fusion.20), channel_id=1, source_target_pairs={{0,16},{16,0},{32,48},{48,32},{64,80},{80,64},{96,112},{112,96},{1... | collective-permute-start | bytes 6291464 | tf_op jit(solution)/shard_map/ppermute | solution.py:28
  508.9 144.0 %slice-start.2 = ((s8[9437184]{0:T(1024)(128)(4,1)}), s8[1048576]{0:T(1024)(128)(4,1)S(1)}, s32[]{:S(2)}) async-start(s8[9437184]{0:T(1024)(128)(4,1)} %bitcast.39), calls=%async_computation.2 | async-start | bytes 2097152
  508.9 46.9 %collective-permute-start.5 = (f32[64,8192]{1,0:T(8,128)S(1)}, f32[64,8192]{1,0:T(8,128)S(1)}, u32[]{:S(2)}, u32[]{:S(2)}) collective-permute-start(f32[64,8192]{1,0:T(8,128)S(1)} %add.52), channel_id=1, source_target_pairs={{0,32},{16,48},{32,0},{48,16},{64,96},{80,112},{96,64},{112,80},{1... | collective-permute-start | bytes 6291464 | tf_op jit(solution)/shard_map/ppermute | solution.py:28
  556.0 93.0 %collective-permute-start.6 = (f32[64,8192]{1,0:T(8,128)S(1)}, f32[64,8192]{1,0:T(8,128)S(1)}, u32[]{:S(2)}, u32[]{:S(2)}) collective-permute-start(f32[64,8192]{1,0:T(8,128)S(1)} %add.53), channel_id=1, source_target_pairs={{0,64},{16,80},{32,96},{48,112},{64,0},{80,16},{96,32},{112,48},{1... | collective-permute-start | bytes 6291464 | tf_op jit(solution)/shard_map/ppermute | solution.py:28
  649.2 96.4 %collective-permute-start.7 = (f32[64,8192]{1,0:T(8,128)S(1)}, f32[64,8192]{1,0:T(8,128)S(1)}, u32[]{:S(2)}, u32[]{:S(2)}) collective-permute-start(f32[64,8192]{1,0:T(8,128)S(1)} %add.54), channel_id=1, source_target_pairs={{0,128},{16,144},{32,160},{48,176},{64,192},{80,208},{96,224},{112... | collective-permute-start | bytes 6291464 | tf_op jit(solution)/shard_map/ppermute | solution.py:28
